TPU v7x, 32 devices: a whole 2x2x4 slice. The times are simulated.
32 devices in a mesh: tm: 8 (over z, y), stream: 4 (over x, core).
Axes of the slice: x: 2, y: 2, z: 4, core: 2. Of those that a mesh axis runs over, the one named last changes fastest.
Arguments:
- signal: bfloat16 [4, 49152, 256], P('stream', 'tm'), may hold values from -6 to 6
- lengths: int32 [4], P('stream'), may hold values from 12288 to 49152, as said below
- w_conv: bfloat16 [512, 512], replicated, may hold values from -0.25 to 0.25
- w_res: bfloat16 [256, 256], replicated, may hold values from -0.375 to 0.375
- w_in: bfloat16 [256, 1024], replicated, may hold values from -0.375 to 0.375
- w_qkv: bfloat16 [1024, 3072], P(None, 'stream')
- w_out: bfloat16 [1024, 1024], P('stream'), may hold values from -0.1875 to 0.1875
- d_out: bfloat16 [4, 192, 1024], P('stream', 'tm'), may hold values from -6 to 6
Outputs:
- out: bfloat16 [4, 192, 1024], P('stream', 'tm')
- d_signal: bfloat16 [4, 49152, 256], P('stream', 'tm')
- g_conv: float32 [512, 512], P('stream')
- g_res: float32 [256, 256], P('stream')
- g_in: float32 [256, 1024], P('stream')
- g_qkv: float32 [1024, 3072], P('tm', 'stream')
- g_out: float32 [1024, 1024], P('stream', 'tm')
Inputs may be any that keep to these rules, and one draw needn't show every extreme that they name: `lengths`: some stay has all 49152 samples valid and some other stay exactly 12288.
All inputs are finite; a program needn't handle non-finite values.
Results may differ from a plain program's by a relative error of at most 0.013.
Values may be sent and summed in bfloat16 or wider, within the bound.
A program may use at most 128 MiB of HBM per device.

v0:
```python
import math
import jax
import jax.numpy as jnp
from jax import lax
from jax.sharding import PartitionSpec as P

HEADS = 16
POOL = 256
DILATION_STEP = 512
EPS = 1e-05
HIGH = lax.Precision.HIGHEST


def shifted(value, axis, by):
    length = lax.axis_size(axis)
    pairs = [(i, i + by) for i in range(length) if 0 <= i + by < length]
    return lax.ppermute(value, axis, pairs)


def neighbour_rows(block, offset):
    return shifted(block, "tm", offset)


def local(signal, lengths, w_conv, w_res, w_in, w_qkv, w_out, d_out):
    stays, sample_values, chans = signal.shape
    width = w_in.shape[1]
    head_size = width // HEADS
    heads_here = w_out.shape[0] // head_size
    toks_here = sample_values // POOL
    scale = 1.0 / math.sqrt(head_size)
    incoming_rows = neighbour_rows(signal[:, sample_values - DILATION_STEP :], 1)
    past_rows = jnp.concatenate([incoming_rows, signal[:, : sample_values - DILATION_STEP]], axis=1)
    joined = jnp.concatenate([past_rows, signal], axis=2)
    mixed = jnp.einsum("bsc,cd->bsd", joined, w_conv, preferred_element_type=jnp.float32)
    tanh_f = jnp.tanh(mixed[..., :chans])
    sig_g = jax.nn.sigmoid(mixed[..., chans:])
    hidden = (tanh_f * sig_g).astype(jnp.bfloat16)
    sample_pos = lax.axis_index("tm") * sample_values + jnp.arange(sample_values, dtype=jnp.int32)
    valid = (sample_pos[None, :] < lengths[:, None])[..., None]
    resid = jnp.where(
        valid,
        signal.astype(jnp.float32)
        + jnp.einsum("bsc,cd->bsd", hidden, w_res, preferred_element_type=jnp.float32),
        0.0,
    )
    pooled = jnp.mean(resid.reshape(stays, toks_here, POOL, chans), axis=2).astype(jnp.bfloat16)
    own_tok = jnp.einsum("btc,cd->btd", pooled, w_in, preferred_element_type=jnp.float32).astype(
        jnp.bfloat16
    )
    group_tok, group_len = (
        lax.all_gather(own_tok, "stream", axis=0, tiled=True),
        lax.all_gather(lengths, "stream", axis=0, tiled=True),
    )
    tok_values = group_tok.astype(jnp.float32)
    tok_scale = lax.rsqrt(jnp.mean(tok_values * tok_values, axis=-1, keepdims=True) + EPS)
    normed = (tok_values * tok_scale).astype(jnp.bfloat16)
    group = normed.shape[0]
    proj = jnp.einsum("btd,de->bte", normed, w_qkv, preferred_element_type=jnp.float32).astype(
        jnp.bfloat16
    )
    proj = proj.reshape(group, toks_here, heads_here, 3, head_size)
    query = proj[:, :, :, 0]
    keyval = proj[:, :, :, 1:].reshape(group, toks_here, heads_here * 2 * head_size)
    all_kv = lax.all_gather(keyval, "tm", axis=1, tiled=True)
    total = all_kv.shape[1]
    all_kv = all_kv.reshape(group, total, heads_here, 2, head_size)
    keys = all_kv[:, :, :, 0]
    values = all_kv[:, :, :, 1]
    query_pos = lax.axis_index("tm") * toks_here + jnp.arange(toks_here, dtype=jnp.int32)
    key_pos = jnp.arange(total, dtype=jnp.int32)
    allowed = (key_pos[None, None, :] <= query_pos[None, :, None]) & (
        (key_pos * POOL)[None, None, :] < group_len[:, None, None]
    )
    scores = jnp.einsum("bqhe,bkhe->bhqk", query, keys, preferred_element_type=jnp.float32) * scale
    scores = jnp.where(allowed[:, None], scores, -1e30)
    top = jnp.max(scores, axis=-1, keepdims=True)
    weights = jnp.exp(scores - top)
    prob = weights / jnp.sum(weights, axis=-1, keepdims=True)
    prob16 = prob.astype(jnp.bfloat16)
    context = jnp.einsum(
        "bhqk,bkhe->bqhe", prob16, values, preferred_element_type=jnp.float32
    ).astype(jnp.bfloat16)
    context = context.reshape(group, toks_here, heads_here * head_size)
    head_part = jnp.einsum("bte,ed->btd", context, w_out, preferred_element_type=jnp.float32)
    summed = lax.psum_scatter(head_part, "stream", scatter_dimension=0, tiled=True)
    out = (own_tok.astype(jnp.float32) + summed).astype(jnp.bfloat16)
    group_grad = lax.all_gather(d_out, "stream", axis=0, tiled=True)
    g_out_part = jnp.einsum("bte,btd->ed", context, group_grad, preferred_element_type=jnp.float32)
    d_context = jnp.einsum(
        "btd,ed->bte", group_grad, w_out, preferred_element_type=jnp.float32
    ).astype(jnp.bfloat16)
    d_context = d_context.reshape(group, toks_here, heads_here, head_size)
    d_prob = jnp.einsum("bqhe,bkhe->bhqk", d_context, values, preferred_element_type=jnp.float32)
    d_score = prob * (d_prob - jnp.sum(d_prob * prob, axis=-1, keepdims=True))
    d_query = scale * jnp.einsum(
        "bhqk,bkhe->bqhe", d_score, keys.astype(jnp.float32), precision=HIGH
    )
    d_keys = scale * jnp.einsum(
        "bhqk,bqhe->bkhe", d_score, query.astype(jnp.float32), precision=HIGH
    )
    d_values = jnp.einsum("bhqk,bqhe->bkhe", prob16, d_context, preferred_element_type=jnp.float32)
    d_kv = jnp.stack([d_keys, d_values], axis=3).reshape(group, total, heads_here * 2 * head_size)
    d_kv_own = lax.psum_scatter(d_kv, "tm", scatter_dimension=1, tiled=True).reshape(
        group, toks_here, heads_here, 2, head_size
    )
    d_proj = jnp.concatenate([d_query[:, :, :, None], d_kv_own], axis=3).reshape(
        group, toks_here, heads_here * 3 * head_size
    )
    g_qkv_part = jnp.einsum("btd,bte->de", normed.astype(jnp.float32), d_proj, precision=HIGH)
    d_normed = jnp.einsum("bte,de->btd", d_proj, w_qkv.astype(jnp.float32), precision=HIGH)
    inner = jnp.sum(d_normed * tok_values, axis=-1, keepdims=True)
    cube = tok_scale * tok_scale * tok_scale
    d_group = tok_scale * d_normed - tok_values * cube * inner / width
    own_grad = d_out.astype(jnp.float32)
    w_in_wide = w_in.astype(jnp.float32)
    d_tok = lax.psum_scatter(d_group, "stream", scatter_dimension=0, tiled=True) + own_grad
    g_in = jnp.einsum("btc,btd->cd", pooled.astype(jnp.float32), d_tok, precision=HIGH)
    d_pooled = jnp.einsum("btd,cd->btc", d_tok, w_in_wide, precision=HIGH)
    spread = jnp.repeat(d_pooled / POOL, POOL, axis=1)
    d_resid = jnp.where(valid, spread, 0.0).astype(jnp.bfloat16)
    g_res = jnp.einsum("bsc,bsd->cd", hidden, d_resid, preferred_element_type=jnp.float32)
    d_hidden = jnp.einsum("bsd,cd->bsc", d_resid, w_res, preferred_element_type=jnp.float32)
    d_mixed = jnp.concatenate(
        [d_hidden * (1.0 - tanh_f * tanh_f) * sig_g, d_hidden * tanh_f * sig_g * (1.0 - sig_g)],
        axis=2,
    ).astype(jnp.bfloat16)
    g_conv = jnp.einsum("bsc,bsd->cd", joined, d_mixed, preferred_element_type=jnp.float32)
    d_joined = jnp.einsum("bsd,cd->bsc", d_mixed, w_conv, preferred_element_type=jnp.float32)
    past_gradient = d_joined[..., :chans].astype(jnp.bfloat16)
    arriving_rows = neighbour_rows(past_gradient[:, :DILATION_STEP], -1)
    later_gradient = jnp.concatenate([past_gradient[:, DILATION_STEP:], arriving_rows], axis=1)
    d_signal = (
        d_resid.astype(jnp.float32) + d_joined[..., chans:] + later_gradient.astype(jnp.float32)
    ).astype(jnp.bfloat16)
    head_qkv, head_out = (
        lax.psum_scatter(g_qkv_part, "tm", scatter_dimension=0, tiled=True),
        lax.psum_scatter(g_out_part, "tm", scatter_dimension=1, tiled=True),
    )
    sum_conv, sum_res, sum_in = lax.psum((g_conv, g_res, g_in), ("tm", "stream"))
    parts = lax.axis_size("stream")
    index = lax.axis_index("stream")
    conv_rows = sum_conv.shape[0] // parts
    res_rows = sum_res.shape[0] // parts
    in_rows = sum_in.shape[0] // parts
    sum_conv = lax.dynamic_slice_in_dim(sum_conv, index * conv_rows, conv_rows, 0)
    sum_res = lax.dynamic_slice_in_dim(sum_res, index * res_rows, res_rows, 0)
    sum_in = lax.dynamic_slice_in_dim(sum_in, index * in_rows, in_rows, 0)
    return (out, d_signal, sum_conv, sum_res, sum_in, head_qkv, head_out)


def solution(mesh):
    in_specs = (
        P("stream", "tm", None),
        P("stream"),
        P(),
        P(),
        P(),
        P(None, "stream"),
        P("stream", None),
        P("stream", "tm", None),
    )
    out_specs = (
        P("stream", "tm", None),
        P("stream", "tm", None),
        P("stream", None),
        P("stream", None),
        P("stream", None),
        P("tm", "stream"),
        P("stream", "tm"),
    )
    return jax.shard_map(local, mesh=mesh, in_specs=in_specs, out_specs=out_specs, check_vma=False)
```

profile of v0, /device:TPU:0, one launch (start us, length us, event | category | flops | bytes accessed | tf_op | source)
XLA Modules:
  0.0 544.1 jit_solution(6773521519445546995)
XLA Ops:
  8.4 4.9 collective-permute-start
  16.0 4.9 all-reduce
  21.0 5.8 %all_gather.15 = bf16[4,24,1024]{2,1,0:T(8,128)(2,1)S(1)} all-gather(bf16[1,24,1024]{2,1,0:T(8,128)(2,1)} %param.15), channel_id=1, replica_groups=mesh['tm'=8,'stream'=4] {'stream'}, dimensions={0}, use_global_device_ids=true | all-gather | bytes 245760 | tf_op jit(solution)/shard_map/all_gather | solution.py:87
  28.8 3.6 slice.38
  32.5 6.5 %convolution_bitcast_fusion.1 = f32[1,6144,512]{1,2,0:T(8,128)S(1)} fusion(bf16[512,512]{1,0:T(8,128)(2,1)S(1)} %copy-done.17, bf16[1,6144,256]{2,1,0:T(8,128)(2,1)} %param.8, bf16[1,5632,256]{2,1,0:T(8,128)(2,1)} %slice.38, bf16[1,512,256]{2,1,0:T(8,128)(2,1)S(1)} %collective-permute-done), kind=kOutput, calls=%fused_computation.3 | convolution fusion | flops 3240099840 | bytes 19398656 | tf_op jit(solution)/shard_map/bsc,cd->bsd/dot_general | solution.py:34
  39.1 2.5 fusion.12
  41.6 2.8 copy-done.7
  44.4 5.3 fusion.3
  49.7 3.3 reduce_sum.45
  53.2 5.6 %all-gather = bf16[96,1024]{1,0:T(8,128)(2,1)S(1)} all-gather(bf16[24,1024]{1,0:T(8,128)(2,1)S(1)} %convolution_convert_fusion.2), channel_id=2, replica_groups=mesh['tm'=8,'stream'=4] {'stream'}, dimensions={0}, use_global_device_ids=true | all-gather | bytes 245760 | tf_op jit(solution)/shard_map/all_gather | solution.py:51
  60.9 32.5 %all_gather.13 = bf16[4,192,512]{2,0,1:T(4,128)(2,1)S(1)} all-gather(bf16[4,24,512]{2,0,1:T(4,128)(2,1)S(1)} %copy.29), channel_id=1, replica_groups=mesh['tm'=8,'stream'=4] {'tm'}, dimensions={1}, use_global_device_ids=true | all-gather | bytes 884736 | tf_op jit(solution)/shard_map/all_gather | solution.py:64
  96.1 2.8 fusion.59
  98.9 1.9 convolution_bitcast_fusion.6
  105.8 2.8 copy.38
  110.2 1.7 fusion.34
  112.8 83.7 %all-reduce.6.cloned.1.call-done = f32[4,192,512]{2,0,1:T(4,128)} async-done(((f32[4,192,512]{2,0,1:T(4,128)}), f32[4,192,512]{2,0,1:T(4,128)}) %all-reduce.6.cloned.1.call-update) | async-done | bytes 1572880
  201.2 2.6 fusion.20
  205.6 1.8 fusion.35
  208.6 17.2 %reduce-scatter.7.cloned.1.call-done = f32[1,24,1024]{2,1,0:T(8,128)} async-done(((f32[4,24,1024]{2,1,0:T(8,128)}), f32[1,24,1024]{2,1,0:T(8,128)}) %reduce-scatter.7.cloned.1.call-update) | async-done | bytes 98320 | tf_op jit(solution)/shard_map/reduce_scatter | solution.py:116
  230.1 5.9 %fusion.16 = f32[256,256]{1,0:T(8,128)} fusion(bf16[6144,256]{0,1:T(8,128)(2,1)} %copy-done.5, bf16[1,6144,1,1,1,1,256]{6,1,5,4,3,2,0:T(8,128)(2,1)S(1)} %bitcast.125, pred[6144]{0:T(1024)(128)(4,1)S(1)} %add_compare_fusion), kind=kOutput, calls=%fused_computation.31 | convolution fusion | flops 806879232 | bytes 6559744 | tf_op jit(solution)/shard_map/bsc,bsd->cd/dot_general | solution.py:121
  236.1 6.8 %fusion.13 = (bf16[6144,256]{0,1:T(8,128)(2,1)S(1)}, bf16[6144,256]{0,1:T(8,128)(2,1)S(1)}) fusion(f32[1,6144,512]{1,2,0:T(8,128)} %copy-done.7, bf16[6144,256]{1,0:T(8,128)(2,1)S(1)} %fusion.9, bf16[256,256]{1,0:T(8,128)(2,1)S(1)} %copy-done.24), kind=kOutput, calls=%fused_computation.28 | convolution fusion | flops 825753600 | bytes 22151168 | tf_op jit(solution)/shard_map/bsd,cd->bsc/dot_general | solution.py:122
  242.9 2.1 fusion.46
  245.9 4.5 fusion.11
  252.2 3.2 convolution_bitcast_fusion.4
  255.4 10.9 %fusion.60 = (bf16[1,6144,512]{2,1,0:T(8,128)(2,1)S(1)}, f32[1,6144,512]{2,1,0:T(8,128)}) fusion(bf16[512,512]{1,0:T(8,128)(2,1)S(1)} %copy-done.18, bf16[6144,256]{0,1:T(8,128)(2,1)} %copy-done.9, bf16[6144,256]{0,1:T(8,128)(2,1)} %copy-done.8), kind=kOutput, calls=%fused_computation.107 | convolution fusion | flops 3236954112 | bytes 25690112 | tf_op jit(solution)/shard_map/bsd,cd->bsc/dot_general | solution.py:128
  266.3 2.6 copy-done.2
  271.8 2.0 slice.55
  273.8 6.1 %collective-permute-done.1 = bf16[1,512,256]{2,1,0:T(8,128)(2,1)S(1)} collective-permute-done((bf16[1,512,256]{2,1,0:T(8,128)(2,1)S(1)}, bf16[1,512,256]{2,1,0:T(8,128)(2,1)S(1)}, u32[]{:S(2)}, u32[]{:S(2)}) %collective-permute-start.1) | collective-permute-done | bytes 262176 | tf_op jit(solution)/shard_map/ppermute | solution.py:17
  279.9 9.5 %fusion.5 = bf16[1,6144,256]{2,1,0:T(8,128)(2,1)} fusion(f32[1,6144,512]{2,1,0:T(8,128)} %get-tuple-element.19, bf16[1,512,256]{2,1,0:T(8,128)(2,1)S(1)} %collective-permute-done.1, bf16[1,5632,256]{2,1,0:T(8,128)(2,1)S(1)} %slice.55, pred[6144]{0:T(1024)(128)(4,1)S(1)} %add_compare_fusion, bf16[1,6144,256]{2,1,0:T(8,128)(2,1)} %bitcast.126), kind=kLoop, calls=%fused_computation.10 | loop fusion | flops 14155776 | bytes 15734784 | tf_op jit(solution)/shard_map/convert_element_type | solution.py:134
  289.4 103.1 %all-reduce.8.cloned.1.call-done = (f32[512,512]{1,0:T(8,128)}, f32[256,256]{1,0:T(8,128)}, f32[256,1024]{1,0:T(8,128)}) async-done(((f32[512,512]{1,0:T(8,128)}, f32[256,256]{1,0:T(8,128)}, f32[256,1024]{1,0:T(8,128)}), (f32[512,512]{1,0:T(8,128)}, f32[256,256]{1,0:T(8,128)}, f32[256,1024]{1,0:T(8,128)})) %all-reduce.8.cloned.1.call-update) | async-done | bytes 2359312 | tf_op jit(solution)/shard_map/psum | solution.py:139
  397.3 62.8 %reduce-scatter.11.cloned.1.call-done = f32[256,128]{1,0:T(8,128)} async-done(((f32[256,1024]{1,0:T(8,128)}), f32[256,128]{1,0:T(8,128)}) %reduce-scatter.11.cloned.1.call-update) | async-done | bytes 131088 | tf_op jit(solution)/shard_map/reduce_scatter | solution.py:137
  460.1 77.2 %reduce-scatter.9.cloned.1.call-done = f32[128,768]{1,0:T(8,128)} async-done(((f32[1024,768]{1,0:T(8,128)}), f32[128,768]{1,0:T(8,128)}) %reduce-scatter.9.cloned.1.call-update) | async-done | bytes 393232 | tf_op jit(solution)/shard_map/reduce_scatter | solution.py:136
  (121 shorter events, 39.4 us)
Async XLA Ops:
  7.2 52.4 %copy-start = (bf16[1024,768]{1,0:T(8,128)(2,1)S(1)}, bf16[1024,768]{1,0:T(8,128)(2,1)}, u32[]{:S(2)}) copy-start(bf16[1024,768]{1,0:T(8,128)(2,1)} %param.13) | copy-start | bytes 4718596
  7.2 25.3 %copy-start.17 = (bf16[512,512]{1,0:T(8,128)(2,1)S(1)}, bf16[512,512]{1,0:T(8,128)(2,1)}, u32[]{:S(2)}) copy-start(bf16[512,512]{1,0:T(8,128)(2,1)} %param.10) | copy-start | bytes 1572868
  7.2 189.3 %all-reduce.6.cloned.1.call-start = ((), (), s32[]{:S(2)}) async-start(), calls=%async_computation.8 | async-start | bytes 3145728
  8.4 24.1 %collective-permute-start = (bf16[1,512,256]{2,1,0:T(8,128)(2,1)S(1)}, bf16[1,512,256]{2,1,0:T(8,128)(2,1)S(1)}, u32[]{:S(2)}, u32[]{:S(2)}) collective-permute-start(bf16[1,512,256]{2,1,0:T(8,128)(2,1)S(1)} %slice.37), channel_id=1, source_target_pairs={{0,4},{4,8},{8,12},{12,16},{16,20},{20,24},{24,28},{1,5},{5,9},{9,... | collective-permute-start | bytes 786440 | tf_op jit(solution)/shard_map/ppermute | solution.py:17
  32.5 6.5 %copy-start.28 = (bf16[1,512,256]{2,1,0:T(8,128)(2,1)}, bf16[1,512,256]{2,1,0:T(8,128)(2,1)S(1)}, u32[]{:S(2)}) copy-start(bf16[1,512,256]{2,1,0:T(8,128)(2,1)S(1)} %collective-permute-done) | copy-start | bytes 786436
  39.1 5.4 copy-start.7
  39.1 5.3 copy-start.3
  39.1 5.3 copy-start.23
  44.4 5.3 copy-start.5
  53.2 6.3 %copy-start.20 = (bf16[24,1024]{1,0:T(8,128)(2,1)}, bf16[24,1024]{1,0:T(8,128)(2,1)S(1)}, u32[]{:S(2)}) copy-start(bf16[24,1024]{1,0:T(8,128)(2,1)S(1)} %convolution_convert_fusion.2) | copy-start | bytes 147460
  59.5 43.4 %copy-start.26 = (f32[4,24]{1,0:T(4,128)}, f32[4,24]{1,0:T(4,128)S(1)}, u32[]{:S(2)}) copy-start(f32[4,24]{1,0:T(4,128)S(1)} %get-tuple-element.13) | copy-start | bytes 1156
  98.9 11.3 %copy-start.25 = (f32[4,4,24]{2,1,0:T(4,128)}, f32[4,4,24]{2,1,0:T(4,128)S(1)}, u32[]{:S(2)}) copy-start(f32[4,4,24]{2,1,0:T(4,128)S(1)} %get-tuple-element.14) | copy-start | bytes 4612
  102.9 6.0 %copy-start.30 = (u32[32]{0:T(128)S(1)}, u32[32]{0:T(128)}, u32[]{:S(2)}) copy-start(u32[32]{0:T(128)} %constant.58) | copy-start | bytes 388
  108.7 117.1 %reduce-scatter.7.cloned.1.call-start = ((), (), s32[]{:S(2)}) async-start(), calls=%async_computation.5 | async-start | bytes 491520 | tf_op jit(solution)/shard_map/reduce_scatter | solution.py:116
  110.2 97.4 %copy-start.11 = (bf16[256,1024]{1,0:T(8,128)(2,1)S(1)}, bf16[256,1024]{1,0:T(8,128)(2,1)}, u32[]{:S(2)}) copy-start(bf16[256,1024]{1,0:T(8,128)(2,1)} %param.14) | copy-start | bytes 1572868
  111.9 113.9 %copy-start.19 = (bf16[1,24,1024]{2,1,0:T(8,128)(2,1)S(1)}, bf16[1,24,1024]{2,1,0:T(8,128)(2,1)}, u32[]{:S(2)}) copy-start(bf16[1,24,1024]{2,1,0:T(8,128)(2,1)} %param.15) | copy-start | bytes 147460
  201.2 24.5 %copy-start.13 = (bf16[256,1024]{1,0:T(8,128)(2,1)S(1)}, bf16[256,1024]{1,0:T(8,128)(2,1)}, u32[]{:S(2)}) copy-start(bf16[256,1024]{1,0:T(8,128)(2,1)} %param.12) | copy-start | bytes 1572868
  205.5 64.7 %reduce-scatter.5.cloned.1.call-start = ((), (), s32[]{:S(2)}) async-start(), calls=%async_computation.4 | async-start | bytes 491520 | tf_op jit(solution)/shard_map/reduce_scatter | solution.py:85
  208.5 184.0 %all-reduce.8.cloned.1.call-start = ((), (), s32[]{:S(2)}) async-start(), calls=%async_computation.9 | async-start | bytes 4718592 | tf_op jit(solution)/shard_map/psum | solution.py:139
  228.2 7.8 %copy-start.24 = (bf16[256,256]{1,0:T(8,128)(2,1)S(1)}, bf16[256,256]{1,0:T(8,128)(2,1)}, u32[]{:S(2)}) copy-start(bf16[256,256]{1,0:T(8,128)(2,1)} %param.11) | copy-start | bytes 393220
  236.1 6.8 %copy-start.22 = (f32[1,24,1024]{2,1,0:T(8,128)S(1)}, f32[1,24,1024]{2,1,0:T(8,128)}, u32[]{:S(2)}) copy-start(f32[1,24,1024]{2,1,0:T(8,128)} %reduce-scatter.7.cloned.1.call-done) | copy-start | bytes 294916
  236.1 9.8 %copy-start.4 = (bf16[1,6144,256]{2,1,0:T(8,128)(2,1)S(1)}, bf16[1,6144,256]{2,1,0:T(8,128)(2,1)}, u32[]{:S(2)}) copy-start(bf16[1,6144,256]{2,1,0:T(8,128)(2,1)} %param.8) | copy-start | bytes 9437188
  236.1 9.8 %copy-start.10 = (bf16[1,5632,256]{2,1,0:T(8,128)(2,1)S(1)}, bf16[1,5632,256]{2,1,0:T(8,128)(2,1)}, u32[]{:S(2)}) copy-start(bf16[1,5632,256]{2,1,0:T(8,128)(2,1)} %slice.38) | copy-start | bytes 8650756
  236.1 9.8 %copy-start.29 = (bf16[1,512,256]{2,1,0:T(8,128)(2,1)S(1)}, bf16[1,512,256]{2,1,0:T(8,128)(2,1)}, u32[]{:S(2)}) copy-start(bf16[1,512,256]{2,1,0:T(8,128)(2,1)} %copy-done.28) | copy-start | bytes 786436
  245.9 6.3 %copy-start.14 = (f32[4,24,768]{2,1,0:T(8,128)S(1)}, f32[4,24,768]{2,1,0:T(8,128)}, u32[]{:S(2)}) copy-start(f32[4,24,768]{2,1,0:T(8,128)} %reshape.321) | copy-start | bytes 884740
  245.9 6.3 %copy-start.27 = (f32[4,24]{1,0:T(4,128)S(1)}, f32[4,24]{1,0:T(4,128)}, u32[]{:S(2)}) copy-start(f32[4,24]{1,0:T(4,128)} %copy-done.26) | copy-start | bytes 1156
  250.4 5.0 copy-start.18
  250.4 209.7 %reduce-scatter.11.cloned.1.call-start = ((), (), s32[]{:S(2)}) async-start(), calls=%async_computation.7 | async-start | bytes 1179648 | tf_op jit(solution)/shard_map/reduce_scatter | solution.py:137
  251.9 285.4 %reduce-scatter.9.cloned.1.call-start = ((), (), s32[]{:S(2)}) async-start(), calls=%async_computation.6 | async-start | bytes 3538944 | tf_op jit(solution)/shard_map/reduce_scatter | solution.py:136
  255.4 14.8 %copy-start.21 = (bf16[24,1024]{1,0:T(8,128)(2,1)S(1)}, bf16[24,1024]{1,0:T(8,128)(2,1)}, u32[]{:S(2)}) copy-start(bf16[24,1024]{1,0:T(8,128)(2,1)} %copy-done.20) | copy-start | bytes 147460
  268.9 11.0 %collective-permute-start.1 = (bf16[1,512,256]{2,1,0:T(8,128)(2,1)S(1)}, bf16[1,512,256]{2,1,0:T(8,128)(2,1)S(1)}, u32[]{:S(2)}, u32[]{:S(2)}) collective-permute-start(bf16[1,512,256]{2,1,0:T(8,128)(2,1)S(1)} %slice.56), channel_id=1, source_target_pairs={{4,0},{8,4},{12,8},{16,12},{20,16},{24,20},{28,24},{5,1},{9,5},{13... | collective-permute-start | bytes 786440 | tf_op jit(solution)/shard_map/ppermute | solution.py:17
  279.9 257.4 %copy-start.1 = (bf16[1024,768]{1,0:T(8,128)(2,1)S(1)}, bf16[1024,768]{1,0:T(8,128)(2,1)}, u32[]{:S(2)}) copy-start(bf16[1024,768]{1,0:T(8,128)(2,1)} %param.13) | copy-start | bytes 4718596
  (7 other events, 17.9 us)
Sparse Core Ops, SparseCore 0:
  108.8 87.6 all-reduce.5
  205.6 20.0 reduce-scatter.6
  228.2 20.8 reduce-scatter.4
  255.4 137.0 all-reduce.7
  396.3 63.7 reduce-scatter.10
  464.1 73.0 reduce-scatter.8
where the time goes:
time: 545 us; the launch traced here: 544 us
  waiting for transfers between devices  350 us (64%)
  matrix products  62.2 us (11%)
  blocking collectives  48.8 us (9%)
  local copies, waits for them, and re-layouts  34.1 us (6%)
  other arithmetic  26.2 us (5%)
  between operations  15.9 us (3%)
  starting transfers between devices  6.85 us (1%)
    psum x1, waiting for transfers between devices, local(): lax.psum((g_conv, g_res, g_in), ('tm', 'stream'))  103 us
    unnamed x7, waiting for transfers between devices  83.8 us
    reduce_scatter x1, waiting for transfers between devices, local(): lax.psum_scatter(g_qkv_part, 'tm', scatter_dimension=0, tiled=True)  77.2 us
    reduce_scatter x1, waiting for transfers between devices, local(): lax.psum_scatter(g_out_part, 'tm', scatter_dimension=1, tiled=True)  62.8 us
    all_gather x1, blocking collectives, local(): all_kv = lax.all_gather(keyval, 'tm', axis=1, tiled=True)  32.5 us
    reduce_scatter x1, waiting for transfers between devices, local(): lax.psum_scatter(d_group, 'stream', scatter_dimension=0, tiled=True)  17.2 us
    unnamed x67, local copies, waits for them, and re-layouts  12.2 us
  transfers between devices with their start and end apart: 8, of which 6 were waited for; matrix products, arithmetic and copies ran while one was open for 13% of the time, Pallas kernels for 0%

commit v1 on v0

--- a/solution.py
+++ b/solution.py
@@ -9,6 +9,11 @@
 DILATION_STEP = 512
 EPS = 1e-05
 HIGH = lax.Precision.HIGHEST
+
+
+def by_each_axis(value_2, axis_one, axis_two):
+    half = lax.psum(value_2, axis_one)
+    return lax.psum(half, axis_two)
 
 
 def shifted(value, axis, by):
@@ -136,7 +141,7 @@
         lax.psum_scatter(g_qkv_part, "tm", scatter_dimension=0, tiled=True),
         lax.psum_scatter(g_out_part, "tm", scatter_dimension=1, tiled=True),
     )
-    sum_conv, sum_res, sum_in = lax.psum((g_conv, g_res, g_in), ("tm", "stream"))
+    sum_conv, sum_res, sum_in = by_each_axis((g_conv, g_res, g_in), "stream", "tm")
     parts = lax.axis_size("stream")
     index = lax.axis_index("stream")
     conv_rows = sum_conv.shape[0] // parts

time: 545 us -> 594 us (1.090)
  waiting for transfers between devices: 350 us -> 400 us
    psum x1 -> x2, waiting for transfers between devices: 103 us -> 152 us  [the longest x1 97.9 us: by_each_axis(): return lax.psum(half, axis_two)]
    unnamed x67 -> x71, local copies, waits for them, and re-layouts: 12.2 us -> 13 us
    unnamed x7 -> x8, waiting for transfers between devices: 83.8 us -> 83.2 us
  transfers between devices with their start and end apart: 8 -> 9, of which waited for: 6 -> 8; matrix products, arithmetic and copies ran while one was open for 13% -> 8% of each run, Pallas kernels for 0% -> 0%
where the time goes in v1:
time: 594 us; the launch traced here: 593 us
  waiting for transfers between devices  400 us (67%)
  matrix products  59 us (10%)
  blocking collectives  48.8 us (8%)
  local copies, waits for them, and re-layouts  36 us (6%)
  other arithmetic  26.5 us (4%)
  between operations  15.9 us (3%)
  starting transfers between devices  6.89 us (1%)
    psum x1, waiting for transfers between devices, by_each_axis(): return lax.psum(half, axis_two)  97.9 us
    unnamed x8, waiting for transfers between devices  83.2 us
    reduce_scatter x1, waiting for transfers between devices, local(): lax.psum_scatter(g_qkv_part, 'tm', scatter_dimension=0, tiled=True)  77.5 us
    reduce_scatter x1, waiting for transfers between devices, local(): lax.psum_scatter(g_out_part, 'tm', scatter_dimension=1, tiled=True)  62.9 us
    psum x1, waiting for transfers between devices, by_each_axis(): half = lax.psum(value_2, axis_one)  53.8 us
    all_gather x1, blocking collectives, local(): all_kv = lax.all_gather(keyval, 'tm', axis=1, tiled=True)  32.5 us
    reduce_scatter x1, waiting for transfers between devices, local(): lax.psum_scatter(d_group, 'stream', scatter_dimension=0, tiled=True)  20.2 us
    unnamed x71, local copies, waits for them, and re-layouts  13 us
  transfers between devices with their start and end apart: 9, of which 8 were waited for; matrix products, arithmetic and copies ran while one was open for 8% of the time, Pallas kernels for 0%

profile of v1, /device:TPU:0, one launch (start us, length us, event | category | flops | bytes accessed | tf_op | source)
XLA Modules:
  0.0 593.3 jit_solution(3739021843453917341)
XLA Ops:
  8.4 4.9 collective-permute-start
  16.0 4.9 all-reduce
  21.0 5.8 all_gather.15
  28.8 3.6 slice.38
  33.2 6.5 %convolution_bitcast_fusion.1 = f32[1,6144,512]{1,2,0:T(8,128)S(1)} fusion(bf16[512,512]{1,0:T(8,128)(2,1)S(1)} %copy-done.18, bf16[1,6144,256]{2,1,0:T(8,128)(2,1)} %param.8, bf16[1,5632,256]{2,1,0:T(8,128)(2,1)} %slice.38, bf16[1,512,256]{2,1,0:T(8,128)(2,1)S(1)} %collective-permute-done), kind=kOutput, calls=%fused_computation.3 | convolution fusion | flops 3240099840 | bytes 19398656 | tf_op jit(solution)/shard_map/bsc,cd->bsd/dot_general | solution.py:39
  39.7 2.5 fusion.12
  42.2 2.8 copy-done.8
  45.1 5.3 fusion.3
  50.4 3.3 reduce_sum.45
  53.9 5.6 all-gather
  62.2 32.5 %all_gather.13 = bf16[4,192,512]{2,0,1:T(4,128)(2,1)S(1)} all-gather(bf16[4,24,512]{2,0,1:T(4,128)(2,1)S(1)} %copy.29), channel_id=1, replica_groups=mesh['tm'=8,'stream'=4] {'tm'}, dimensions={1}, use_global_device_ids=true | all-gather | bytes 884736 | tf_op jit(solution)/shard_map/all_gather | solution.py:69
  97.5 2.8 fusion.59
  100.3 2.8 convolution_bitcast_fusion.6
  104.5 1.7 fusion.24
  109.1 2.8 copy.38
  116.6 83.0 %all-reduce.8.cloned.1.call-done = f32[4,192,512]{2,0,1:T(4,128)} async-done(((f32[4,192,512]{2,0,1:T(4,128)}), f32[4,192,512]{2,0,1:T(4,128)}) %all-reduce.8.cloned.1.call-update) | async-done | bytes 1572880
  204.4 2.5 fusion.20
  208.6 20.2 %reduce-scatter.7.cloned.1.call-done = f32[1,24,1024]{2,1,0:T(8,128)} async-done(((f32[4,24,1024]{2,1,0:T(8,128)}), f32[1,24,1024]{2,1,0:T(8,128)}) %reduce-scatter.7.cloned.1.call-update) | async-done | bytes 98320 | tf_op jit(solution)/shard_map/reduce_scatter | solution.py:121
  233.4 1.8 fusion.16
  235.2 6.8 %fusion.13 = (bf16[6144,256]{0,1:T(8,128)(2,1)S(1)}, bf16[6144,256]{0,1:T(8,128)(2,1)S(1)}) fusion(f32[1,6144,512]{1,2,0:T(8,128)} %copy-done.8, bf16[6144,256]{1,0:T(8,128)(2,1)S(1)} %fusion.9, bf16[256,256]{1,0:T(8,128)(2,1)S(1)} %copy-done.25), kind=kOutput, calls=%fused_computation.28 | convolution fusion | flops 825753600 | bytes 22151168 | tf_op jit(solution)/shard_map/bsd,cd->bsc/dot_general | solution.py:127
  242.0 2.0 fusion.46
  245.0 4.5 fusion.11
  251.6 53.8 %all-reduce.12.cloned.1.call-done = (f32[512,512]{1,0:T(8,128)}, f32[256,256]{1,0:T(8,128)}, f32[256,1024]{1,0:T(8,128)}) async-done(((f32[512,512]{1,0:T(8,128)}, f32[256,256]{1,0:T(8,128)}, f32[256,1024]{1,0:T(8,128)}), (f32[512,512]{1,0:T(8,128)}, f32[256,256]{1,0:T(8,128)}, f32[256,1024]{1,0:T(8,128)})) %all-reduce.12.cloned.1.call-update) | async-done | bytes 2359312 | tf_op jit(solution)/shard_map/psum | solution.py:15
  307.1 3.2 convolution_bitcast_fusion.4
  310.4 10.9 %fusion.60 = (bf16[1,6144,512]{2,1,0:T(8,128)(2,1)S(1)}, f32[1,6144,512]{2,1,0:T(8,128)}) fusion(bf16[512,512]{1,0:T(8,128)(2,1)S(1)} %copy-done.19, bf16[6144,256]{0,1:T(8,128)(2,1)} %copy-done.10, bf16[6144,256]{0,1:T(8,128)(2,1)} %copy-done.9), kind=kOutput, calls=%fused_computation.107 | convolution fusion | flops 3236954112 | bytes 25690112 | tf_op jit(solution)/shard_map/bsd,cd->bsc/dot_general | solution.py:133
  321.2 2.6 copy-done.2
  325.2 3.5 reduce-scatter.5.cloned.1.call-done
  330.2 2.0 slice.55
  333.5 9.8 %fusion.5 = bf16[1,6144,256]{2,1,0:T(8,128)(2,1)} fusion(f32[1,6144,512]{2,1,0:T(8,128)} %get-tuple-element.22, bf16[1,512,256]{2,1,0:T(8,128)(2,1)S(1)} %collective-permute-done.1, bf16[1,5632,256]{2,1,0:T(8,128)(2,1)S(1)} %slice.55, pred[6144]{0:T(1024)(128)(4,1)S(1)} %add_compare_fusion, bf16[1,6144,256]{2,1,0:T(8,128)(2,1)} %bitcast.126), kind=kLoop, calls=%fused_computation.10 | loop fusion | flops 14155776 | bytes 15734784 | tf_op jit(solution)/shard_map/convert_element_type | solution.py:139
  343.3 97.9 %all-reduce.10.cloned.1.call-done = (f32[512,512]{1,0:T(8,128)}, f32[256,256]{1,0:T(8,128)}, f32[256,1024]{1,0:T(8,128)}) async-done(((f32[512,512]{1,0:T(8,128)}, f32[256,256]{1,0:T(8,128)}, f32[256,1024]{1,0:T(8,128)}), (f32[512,512]{1,0:T(8,128)}, f32[256,256]{1,0:T(8,128)}, f32[256,1024]{1,0:T(8,128)})) %all-reduce.10.cloned.1.call-update) | async-done | bytes 2359312 | tf_op jit(solution)/shard_map/psum | solution.py:16
  446.1 62.9 %reduce-scatter.11.cloned.1.call-done = f32[256,128]{1,0:T(8,128)} async-done(((f32[256,1024]{1,0:T(8,128)}), f32[256,128]{1,0:T(8,128)}) %reduce-scatter.11.cloned.1.call-update) | async-done | bytes 131088 | tf_op jit(solution)/shard_map/reduce_scatter | solution.py:142
  508.9 77.5 %reduce-scatter.9.cloned.1.call-done = f32[128,768]{1,0:T(8,128)} async-done(((f32[1024,768]{1,0:T(8,128)}), f32[128,768]{1,0:T(8,128)}) %reduce-scatter.9.cloned.1.call-update) | async-done | bytes 393232 | tf_op jit(solution)/shard_map/reduce_scatter | solution.py:141
  (128 shorter events, 44.7 us)
Async XLA Ops:
  7.2 53.0 %copy-start = (bf16[1024,768]{1,0:T(8,128)(2,1)S(1)}, bf16[1024,768]{1,0:T(8,128)(2,1)}, u32[]{:S(2)}) copy-start(bf16[1024,768]{1,0:T(8,128)(2,1)} %param.13) | copy-start | bytes 4718596
  7.2 26.0 %copy-start.18 = (bf16[512,512]{1,0:T(8,128)(2,1)S(1)}, bf16[512,512]{1,0:T(8,128)(2,1)}, u32[]{:S(2)}) copy-start(bf16[512,512]{1,0:T(8,128)(2,1)} %param.10) | copy-start | bytes 1572868
  7.2 192.4 %all-reduce.8.cloned.1.call-start = ((), (), s32[]{:S(2)}) async-start(), calls=%async_computation.8 | async-start | bytes 3145728
  8.4 24.8 %collective-permute-start = (bf16[1,512,256]{2,1,0:T(8,128)(2,1)S(1)}, bf16[1,512,256]{2,1,0:T(8,128)(2,1)S(1)}, u32[]{:S(2)}, u32[]{:S(2)}) collective-permute-start(bf16[1,512,256]{2,1,0:T(8,128)(2,1)S(1)} %slice.37), channel_id=1, source_target_pairs={{0,4},{4,8},{8,12},{12,16},{16,20},{20,24},{24,28},{1,5},{5,9},{9,... | collective-permute-start | bytes 786440 | tf_op jit(solution)/shard_map/ppermute | solution.py:22
  33.1 6.5 %copy-start.31 = (bf16[1,512,256]{2,1,0:T(8,128)(2,1)}, bf16[1,512,256]{2,1,0:T(8,128)(2,1)S(1)}, u32[]{:S(2)}) copy-start(bf16[1,512,256]{2,1,0:T(8,128)(2,1)S(1)} %collective-permute-done) | copy-start | bytes 786436
  39.7 5.4 copy-start.8
  39.7 5.3 copy-start.3
  39.7 5.3 copy-start.24
  45.0 5.3 copy-start.5
  53.9 6.3 %copy-start.21 = (bf16[24,1024]{1,0:T(8,128)(2,1)}, bf16[24,1024]{1,0:T(8,128)(2,1)S(1)}, u32[]{:S(2)}) copy-start(bf16[24,1024]{1,0:T(8,128)(2,1)S(1)} %convolution_convert_fusion.2) | copy-start | bytes 147460
  60.2 46.0 %copy-start.28 = (f32[4,24]{1,0:T(4,128)}, f32[4,24]{1,0:T(4,128)S(1)}, u32[]{:S(2)}) copy-start(f32[4,24]{1,0:T(4,128)S(1)} %get-tuple-element.16) | copy-start | bytes 1156
  100.3 8.8 %copy-start.26 = (f32[4,4,24]{2,1,0:T(4,128)}, f32[4,4,24]{2,1,0:T(4,128)S(1)}, u32[]{:S(2)}) copy-start(f32[4,4,24]{2,1,0:T(4,128)S(1)} %get-tuple-element.17) | copy-start | bytes 4612
  111.9 116.9 %copy-start.20 = (bf16[1,24,1024]{2,1,0:T(8,128)(2,1)S(1)}, bf16[1,24,1024]{2,1,0:T(8,128)(2,1)}, u32[]{:S(2)}) copy-start(bf16[1,24,1024]{2,1,0:T(8,128)(2,1)} %param.15) | copy-start | bytes 147460
  111.9 116.9 %reduce-scatter.7.cloned.1.call-start = ((), (), s32[]{:S(2)}) async-start(), calls=%async_computation.5 | async-start | bytes 491520 | tf_op jit(solution)/shard_map/reduce_scatter | solution.py:121
  208.6 96.8 %all-reduce.12.cloned.1.call-start = ((), (), s32[]{:S(2)}) async-start(), calls=%async_computation.10 | async-start | bytes 4718592 | tf_op jit(solution)/shard_map/psum | solution.py:15
  235.2 6.8 %copy-start.23 = (f32[1,24,1024]{2,1,0:T(8,128)S(1)}, f32[1,24,1024]{2,1,0:T(8,128)}, u32[]{:S(2)}) copy-start(f32[1,24,1024]{2,1,0:T(8,128)} %reduce-scatter.7.cloned.1.call-done) | copy-start | bytes 294916
  235.2 9.8 %copy-start.4 = (bf16[1,6144,256]{2,1,0:T(8,128)(2,1)S(1)}, bf16[1,6144,256]{2,1,0:T(8,128)(2,1)}, u32[]{:S(2)}) copy-start(bf16[1,6144,256]{2,1,0:T(8,128)(2,1)} %param.8) | copy-start | bytes 9437188
  235.2 9.8 %copy-start.11 = (bf16[1,5632,256]{2,1,0:T(8,128)(2,1)S(1)}, bf16[1,5632,256]{2,1,0:T(8,128)(2,1)}, u32[]{:S(2)}) copy-start(bf16[1,5632,256]{2,1,0:T(8,128)(2,1)} %slice.38) | copy-start | bytes 8650756
  235.2 9.8 %copy-start.32 = (bf16[1,512,256]{2,1,0:T(8,128)(2,1)S(1)}, bf16[1,512,256]{2,1,0:T(8,128)(2,1)}, u32[]{:S(2)}) copy-start(bf16[1,512,256]{2,1,0:T(8,128)(2,1)} %copy-done.31) | copy-start | bytes 786436
  245.0 4.6 copy-start.27
  245.0 5.5 copy-start.14
  249.5 55.9 %copy-start.17 = (bf16[4,24,1024]{2,1,0:T(8,128)(2,1)S(1)}, bf16[4,24,1024]{2,1,0:T(8,128)(2,1)}, u32[]{:S(2)}) copy-start(bf16[4,24,1024]{2,1,0:T(8,128)(2,1)} %copy-done.16) | copy-start | bytes 589828
  249.5 57.6 %copy-start.15 = (f32[4,24,768]{2,1,0:T(8,128)S(1)}, f32[4,24,768]{2,1,0:T(8,128)}, u32[]{:S(2)}) copy-start(f32[4,24,768]{2,1,0:T(8,128)} %reshape.321) | copy-start | bytes 884740
  249.5 57.6 %copy-start.29 = (f32[4,24]{1,0:T(4,128)S(1)}, f32[4,24]{1,0:T(4,128)}, u32[]{:S(2)}) copy-start(f32[4,24]{1,0:T(4,128)} %copy-done.28) | copy-start | bytes 1156
  249.6 79.1 %reduce-scatter.5.cloned.1.call-start = ((), (), s32[]{:S(2)}) async-start(), calls=%async_computation.4 | async-start | bytes 491520 | tf_op jit(solution)/shard_map/reduce_scatter | solution.py:90
  251.6 58.8 %copy-start.19 = (bf16[512,512]{1,0:T(8,128)(2,1)S(1)}, bf16[512,512]{1,0:T(8,128)(2,1)}, u32[]{:S(2)}) copy-start(bf16[512,512]{1,0:T(8,128)(2,1)} %param.10) | copy-start | bytes 1572868
  251.6 189.7 %all-reduce.10.cloned.1.call-start = ((), (), s32[]{:S(2)}) async-start(), calls=%async_computation.9 | async-start | bytes 4718592 | tf_op jit(solution)/shard_map/psum | solution.py:16
  305.4 203.5 %reduce-scatter.11.cloned.1.call-start = ((), (), s32[]{:S(2)}) async-start(), calls=%async_computation.7 | async-start | bytes 1179648 | tf_op jit(solution)/shard_map/reduce_scatter | solution.py:142
  306.9 279.6 %reduce-scatter.9.cloned.1.call-start = ((), (), s32[]{:S(2)}) async-start(), calls=%async_computation.6 | async-start | bytes 3538944 | tf_op jit(solution)/shard_map/reduce_scatter | solution.py:141
  310.4 18.3 %copy-start.22 = (bf16[24,1024]{1,0:T(8,128)(2,1)S(1)}, bf16[24,1024]{1,0:T(8,128)(2,1)}, u32[]{:S(2)}) copy-start(bf16[24,1024]{1,0:T(8,128)(2,1)} %copy-done.21) | copy-start | bytes 147460
  323.9 9.7 %collective-permute-start.1 = (bf16[1,512,256]{2,1,0:T(8,128)(2,1)S(1)}, bf16[1,512,256]{2,1,0:T(8,128)(2,1)S(1)}, u32[]{:S(2)}, u32[]{:S(2)}) collective-permute-start(bf16[1,512,256]{2,1,0:T(8,128)(2,1)S(1)} %slice.56), channel_id=1, source_target_pairs={{4,0},{8,4},{12,8},{16,12},{20,16},{24,20},{28,24},{5,1},{9,5},{13... | collective-permute-start | bytes 786440 | tf_op jit(solution)/shard_map/ppermute | solution.py:22
  333.5 252.9 %copy-start.1 = (bf16[1024,768]{1,0:T(8,128)(2,1)S(1)}, bf16[1024,768]{1,0:T(8,128)(2,1)}, u32[]{:S(2)}) copy-start(bf16[1024,768]{1,0:T(8,128)(2,1)} %param.13) | copy-start | bytes 4718596
  (10 other events, 30.8 us)
Sparse Core Ops, SparseCore 0:
  112.0 87.5 all-reduce.7
  208.7 20.0 reduce-scatter.6
  249.7 55.6 all-reduce.11
  307.7 20.8 reduce-scatter.4
  332.4 108.7 all-reduce.9
  445.1 63.8 reduce-scatter.10
  513.1 73.2 reduce-scatter.8
